TPU v7x, 256 devices: a whole 4x4x8 slice. The times are simulated.
256 devices in a mesh: rows: 64 (over z, y, core), rep: 4 (over x).
Axes of the slice: x: 4, y: 4, z: 8, core: 2. Of those that a mesh axis runs over, the one named last changes fastest.
Arguments:
- features: bfloat16 [262144, 256], P(('rows', 'rep')), may hold values from -6 to 6
- weight: bfloat16 [256, 256], replicated, may hold values from -0.375 to 0.375
- block_cols: int32 [2048, 4, 2], P('rows', 'rep'), may hold values from 0 to 511, as said below
- block_vals: bfloat16 [2048, 4, 2, 128, 128], P('rows', 'rep'), as said below
- out_grad: bfloat16 [262144, 256], P('rows'), may hold values from -6 to 6
Outputs:
- activations: bfloat16 [262144, 256], P(('rows', 'rep'))
- input_grad: bfloat16 [262144, 256], P(('rows', 'rep'))
- weight_grad: float32 [256, 256], replicated
Inputs may be any that keep to these rules, and one draw needn't show every extreme that they name: `block_cols`: layer c's k-th block column is global block column (k // 8) * 32 + c * 8 + k % 8, whose rows the device of index k // 8 along rows holds in layer c. In the layer that owns a block row, slot 0 is its diagonal block; no other held block of a device lies in its own block columns. For every layer, every device along rows and every other device along rows, at most 1 of the first device's held blocks in that layer lie in block columns of the other, and in every draw some pair has exactly 1. `block_vals`: the adjacency is symmetric: every held block at block row b, block column g in slot s has a partner held at block row g, block column b in slot s (of the layer owning b) that is its transpose; diagonal blocks are symmetric.
All inputs are finite; a program needn't handle non-finite values.
Results may differ from a plain program's by a relative error of at most 0.006.
Values may be sent and summed in bfloat16 or wider, within the bound.
A program may use at most 128 MiB of HBM per device.

v0:
```python
import math
import jax
import jax.numpy as jnp
from jax import lax
from jax.sharding import PartitionSpec as P


def silu_parts(summed):
    sigmoid_vals = jax.nn.sigmoid(summed)
    return (summed * sigmoid_vals, sigmoid_vals * (1.0 + summed * (1.0 - sigmoid_vals)))


def apply_blocks(local_vals, fetched):
    product = jnp.einsum("bsij,bsjf->bif", local_vals, fetched, preferred_element_type=jnp.float32)
    return product.reshape(-1, fetched.shape[-1])


def serve_blocks(source_rows, asked_places, block_size):
    feature_width = source_rows.shape[1]
    blocks = source_rows.reshape(-1, block_size, feature_width)
    flat_ask = asked_places.reshape(-1)
    picked = jnp.take(blocks, jnp.clip(flat_ask, 0, blocks.shape[0] - 1), axis=0)
    picked = jnp.where((flat_ask >= 0)[:, None, None], picked, jnp.zeros_like(picked))
    return picked


def on_device(features, weight, block_cols, block_vals, out_grad):
    own_rows, feature_width = features.shape
    block_size = block_vals.shape[-1]
    row_blocks, slot_count = (block_cols.shape[0], block_cols.shape[2])
    own_blocks = own_rows // block_size
    peer_count = lax.axis_size("rows")
    layer_count = lax.axis_size("rep")
    couple_total = ((layer_count - 1) * slot_count * own_blocks + own_blocks) // 2
    reach_classes = peer_count // 2 - 1
    capacity = (couple_total + reach_classes - 1) // reach_classes
    my_group = lax.axis_index("rows")
    layer_index = lax.axis_index("rep")
    local_vals = block_vals[:, 0]
    flat_cols = block_cols[:, 0].reshape(-1)
    request_total = flat_cols.shape[0]
    owners = flat_cols // own_blocks
    places = flat_cols % own_blocks
    remote = owners != my_group
    positions = jnp.arange(request_total, dtype=jnp.int32)
    same_owner = (owners[:, None] == owners[None, :]) & (positions[:, None] > positions[None, :])
    owner_ranks = jnp.sum(same_owner.astype(jnp.int32), axis=1)
    slot_keys = jnp.where(remote, owners * capacity + owner_ranks, -1)
    slot_table = jnp.arange(peer_count * capacity, dtype=jnp.int32)
    matches = slot_keys[:, None] == slot_table[None, :]
    requests = (jnp.sum(jnp.where(matches, places[:, None] + 1, 0), axis=0) - 1).reshape(
        peer_count, capacity
    )
    asked_places = lax.all_to_all(requests, "rows", split_axis=0, concat_axis=0, tiled=True)
    mixed_rows = jnp.dot(features, weight, preferred_element_type=jnp.float32).astype(jnp.bfloat16)
    arrived = lax.all_to_all(
        serve_blocks(mixed_rows, asked_places, block_size),
        "rows",
        split_axis=0,
        concat_axis=0,
        tiled=True,
    )
    from_peers = jnp.take(arrived, jnp.clip(slot_keys, 0, arrived.shape[0] - 1), axis=0)
    from_self = jnp.take(mixed_rows.reshape(own_blocks, block_size, feature_width), places, axis=0)
    joined = jnp.where(remote[:, None, None], from_peers, from_self)
    partial_sum = apply_blocks(
        local_vals, joined.reshape(row_blocks, slot_count, block_size, feature_width)
    )
    share_start = layer_index * own_rows
    summed = lax.psum(partial_sum, "rep")
    values_all, slopes_all = silu_parts(summed)
    grad_rows = (out_grad.astype(jnp.float32) * slopes_all).astype(jnp.bfloat16)
    activated = lax.dynamic_slice_in_dim(values_all, share_start, own_rows, 0).astype(jnp.bfloat16)
    slot_terms = jnp.einsum(
        "bsji,bjf->bsif",
        local_vals,
        grad_rows.reshape(row_blocks, block_size, feature_width),
        preferred_element_type=jnp.float32,
    ).reshape(request_total, block_size, feature_width)
    filler = jnp.sum(jnp.where(matches, positions[:, None], 0), axis=0)
    filled = jnp.any(matches, axis=0)
    outgoing = jnp.where(
        filled[:, None, None], jnp.take(slot_terms, filler, axis=0), jnp.zeros((), jnp.float32)
    )
    returned = lax.all_to_all(outgoing, "rows", split_axis=0, concat_axis=0, tiled=True)
    block_span = block_size * feature_width
    own_index = jnp.arange(own_blocks, dtype=jnp.int32)
    arrive_hot = (asked_places.reshape(-1)[:, None] == own_index[None, :]).astype(jnp.float32)
    self_hot = ((~remote)[:, None] & (places[:, None] == own_index[None, :])).astype(jnp.float32)
    collected = jnp.einsum(
        "qo,qx->ox", arrive_hot, returned.reshape(-1, block_span), precision=lax.Precision.HIGHEST
    )
    self_terms = jnp.einsum(
        "no,nx->ox", self_hot, slot_terms.reshape(-1, block_span), precision=lax.Precision.HIGHEST
    )
    back_rows = (collected + self_terms).reshape(own_rows, feature_width)
    node_total = own_rows * peer_count * layer_count
    local_weight = jnp.dot(
        features.astype(jnp.float32).T, back_rows, precision=lax.Precision.HIGHEST
    )
    weight_grad = lax.psum(local_weight, ("rows", "rep")) * (1.0 / math.sqrt(node_total))
    input_grad = jnp.dot(
        back_rows.astype(jnp.bfloat16), weight.T, preferred_element_type=jnp.float32
    ).astype(jnp.bfloat16)
    return (activated, input_grad, weight_grad)


def solution(mesh):
    placed = (
        P(("rows", "rep"), None),
        P(),
        P("rows", "rep", None),
        P("rows", "rep", None, None, None),
        P("rows", None),
    )
    return jax.shard_map(
        on_device,
        mesh=mesh,
        in_specs=placed,
        out_specs=(P(("rows", "rep"), None), P(("rows", "rep"), None), P()),
        check_vma=False,
    )
```

profile of v0, /device:TPU:2, one launch (start us, length us, event | category | flops | bytes accessed | tf_op | source)
XLA Modules:
  0.0 755.1 jit_solution(3216159301547902736)
XLA Ops:
  9.3 12.1 %all-to-all-start = ((s32[64,1,1]{2,1,0:T(1,128)}), s32[64,1,1]{2,1,0:T(1,128)S(1)}, u32[]{:S(2)}, u32[]{:S(2)}) async-start(s32[64,1,1]{2,1,0:T(1,128)} %copy.38), calls=%async_computation | async-start | bytes 65536 | tf_op jit(solution)/shard_map/all_to_all | solution.py:54
  22.7 8.2 %all-to-all-done = s32[64,1,1]{2,1,0:T(1,128)S(1)} async-done(((s32[64,1,1]{2,1,0:T(1,128)}), s32[64,1,1]{2,1,0:T(1,128)S(1)}, u32[]{:S(2)}, u32[]{:S(2)}) %all-to-all-start) | async-done | bytes 288 | tf_op jit(solution)/shard_map/all_to_all | solution.py:54
  32.1 2.8 gather_fusion.2
  36.1 4.0 select_select_fusion.2
  40.1 5.7 all-to-all-start.1
  46.1 2.8 gather_fusion.3
  48.9 93.1 %all-to-all-done.1 = bf16[64,128,256]{2,1,0:T(8,128)(2,1)} async-done(((bf16[64,128,256]{2,1,0:T(8,128)(2,1)}), bf16[64,128,256]{2,1,0:T(8,128)(2,1)}, u32[]{:S(2)}, u32[]{:S(2)}) %all-to-all-start.1) | async-done | bytes 4194336 | tf_op jit(solution)/shard_map/all_to_all | solution.py:56
  142.0 5.0 gather_fusion
  147.0 4.1 select_select_fusion.1
  151.0 2.8 fusion.2
  154.0 92.9 %all-reduce.3.cloned.1.call-done = f32[4096,256]{1,0:T(8,128)} async-done(((f32[4096,256]{1,0:T(8,128)}), f32[4096,256]{1,0:T(8,128)}) %all-reduce.3.cloned.1.call-update) | async-done | bytes 4194320 | tf_op jit(solution)/shard_map/psum | solution.py:70
  246.9 6.4 multiply_convert_fusion
  253.3 4.5 fusion
  257.9 9.0 %copy.41 = f32[64,128,256]{2,1,0:T(8,128)} copy(f32[64,128,256]{1,2,0:T(8,128)} %bitcast.59) | data formatting | bytes 16777216 | tf_op jit(solution)/shard_map/reshape | solution.py:79
  266.9 7.7 %gather_fusion.1 = f32[64,128,256]{2,1,0:T(8,128)} fusion(f32[64,128,256]{2,1,0:T(8,128)} %copy.41, s32[1024]{0:T(1024)S(1)} %pad_clamp_fusion), kind=kCustom, calls=%fused_computation.3 | custom fusion | bytes 16777472 | tf_op jit(solution)/shard_map/jit(_take)/gather | solution.py:83
  274.5 8.5 %select_select_fusion = f32[64,128,256]{2,1,0:T(8,128)} fusion(f32[64,128,256]{2,1,0:T(8,128)} %gather_fusion.1, pred[64]{0:T(512)(128)(4,1)S(1)} %compare_and_fusion.2, pred[64]{0:T(512)(128)(4,1)S(1)} %fusion.6), kind=kLoop, calls=%fused_computation.5 | loop fusion | flops 4194304 | bytes 16777344 | tf_op jit(solution)/shard_map/jit(_where)/select_n | solution.py:82
  283.0 10.7 %all-to-all-start.2 = ((f32[64,128,256]{2,1,0:T(8,128)}), f32[64,128,256]{2,1,0:T(8,128)}, u32[]{:S(2)}, u32[]{:S(2)}) async-start(f32[64,128,256]{2,1,0:T(8,128)} %select_select_fusion), calls=%async_computation.2 | async-start | bytes 16777216 | tf_op jit(solution)/shard_map/all_to_all | solution.py:85
  293.8 9.2 %copy.49 = f32[8,8,128,256]{3,1,2,0:T(8,128)} copy(f32[8,8,128,256]{2,3,1,0:T(8,128)} %bitcast.60) | data formatting | bytes 16777216
  305.5 174.4 %all-to-all-done.2 = f32[64,128,256]{2,1,0:T(8,128)} async-done(((f32[64,128,256]{2,1,0:T(8,128)}), f32[64,128,256]{2,1,0:T(8,128)}, u32[]{:S(2)}, u32[]{:S(2)}) %all-to-all-start.2) | async-done | bytes 8388640 | tf_op jit(solution)/shard_map/all_to_all | solution.py:85
  479.9 8.3 %copy.48 = f32[8,8,128,256]{3,1,2,0:T(8,128)S(1)} copy(f32[8,8,128,256]{3,2,1,0:T(8,128)} %bitcast.25) | data formatting | bytes 16777216
  488.1 2.9 fusion.8
  491.1 3.9 convolution_add_fusion
  496.4 2.7 convolution_bitcast_fusion
  500.3 246.2 %all-reduce.5.cloned.1.call-done = f32[256,256]{0,1:T(8,128)} async-done(((f32[256,256]{0,1:T(8,128)}), f32[256,256]{0,1:T(8,128)}) %all-reduce.5.cloned.1.call-update) | async-done | bytes 262160 | tf_op jit(solution)/shard_map/psum | solution.py:101
  (42 shorter events, 13.2 us)
Async XLA Ops:
  7.2 143.9 %copy-start = (bf16[32,1,2,128,128]{4,3,2,1,0:T(8,128)(2,1)S(1)}, bf16[32,1,2,128,128]{4,3,2,1,0:T(8,128)(2,1)}, u32[]{:S(2)}) copy-start(bf16[32,1,2,128,128]{4,3,2,1,0:T(8,128)(2,1)} %param.10) | copy-start | bytes 6291460
  9.3 21.6 %all-to-all-start = ((s32[64,1,1]{2,1,0:T(1,128)}), s32[64,1,1]{2,1,0:T(1,128)S(1)}, u32[]{:S(2)}, u32[]{:S(2)}) async-start(s32[64,1,1]{2,1,0:T(1,128)} %copy.38), calls=%async_computation | async-start | bytes 65536 | tf_op jit(solution)/shard_map/all_to_all | solution.py:54
  40.1 101.9 %all-to-all-start.1 = ((bf16[64,128,256]{2,1,0:T(8,128)(2,1)}), bf16[64,128,256]{2,1,0:T(8,128)(2,1)}, u32[]{:S(2)}, u32[]{:S(2)}) async-start(bf16[64,128,256]{2,1,0:T(8,128)(2,1)} %select_select_fusion.2), calls=%async_computation.1 | async-start | bytes 8388608 | tf_op jit(solution)/shard_map/all_to_all | solution.py:56
  45.8 201.1 %all-reduce.3.cloned.1.call-start = ((), (), s32[]{:S(2)}) async-start(), calls=%async_computation.3 | async-start | bytes 8388608 | tf_op jit(solution)/shard_map/psum | solution.py:70
  283.0 196.8 %all-to-all-start.2 = ((f32[64,128,256]{2,1,0:T(8,128)}), f32[64,128,256]{2,1,0:T(8,128)}, u32[]{:S(2)}, u32[]{:S(2)}) async-start(f32[64,128,256]{2,1,0:T(8,128)} %select_select_fusion), calls=%async_computation.2 | async-start | bytes 16777216 | tf_op jit(solution)/shard_map/all_to_all | solution.py:85
  293.8 452.7 %all-reduce.5.cloned.1.call-start = ((), (), s32[]{:S(2)}) async-start(), calls=%async_computation.4 | async-start | bytes 524288 | tf_op jit(solution)/shard_map/psum | solution.py:101
  479.8 11.2 %slice-start = ((s8[8388608]{0:T(1024)(128)(4,1)}), s8[4194304]{0:T(1024)(128)(4,1)S(1)}, s32[]{:S(2)}) async-start(s8[8388608]{0:T(1024)(128)(4,1)} %bitcast.63), calls=%async_computation.5 | async-start | bytes 8388608
  479.9 11.2 %slice-start.1 = ((s8[8388608]{0:T(1024)(128)(4,1)}), s8[4194304]{0:T(1024)(128)(4,1)S(1)}, s32[]{:S(2)}) async-start(s8[8388608]{0:T(1024)(128)(4,1)} %bitcast.63), calls=%async_computation.6 | async-start | bytes 8388608
  491.0 257.2 %copy-start.1 = (bf16[32,1,2,128,128]{4,3,2,1,0:T(8,128)(2,1)S(1)}, bf16[32,1,2,128,128]{4,3,2,1,0:T(8,128)(2,1)}, u32[]{:S(2)}) copy-start(bf16[32,1,2,128,128]{4,3,2,1,0:T(8,128)(2,1)} %param.10) | copy-start | bytes 6291460
  494.9 4.2 copy-start.2
Sparse Core Ops, SparseCore 0:
  154.0 92.8 all-reduce.2
  499.2 247.1 all-reduce.4
where the time goes:
time: 756 us; the launch traced here: 755 us
  waiting for transfers between devices  615 us (81%)
  local copies, waits for them, and re-layouts  48.7 us (6%)
  other arithmetic  29.3 us (4%)
  starting transfers between devices  28.8 us (4%)
  matrix products  19.3 us (3%)
  between operations  14.2 us (2%)
    psum x1, waiting for transfers between devices, on_device(): lax.psum(local_weight, ('rows', 'rep')) * (1.0 / math.sqrt(node_total))  246 us
    all_to_all x1, waiting for transfers between devices, on_device(): lax.all_to_all(outgoing, 'rows', split_axis=0, concat_axis=0, tiled=True)  174 us
    all_to_all x1, waiting for transfers between devices, on_device(): lax.all_to_all(serve_blocks(mixed_rows, asked_places, block_size), 'rows'...  93.1 us
    psum x1, waiting for transfers between devices, on_device(): summed = lax.psum(partial_sum, 'rep')  92.9 us
    unnamed x14, local copies, waits for them, and re-layouts  19.2 us
  transfers between devices with their start and end apart: 5, of which 5 were waited for; matrix products, arithmetic and copies ran while one was open for 2% of the time, Pallas kernels for 0%

commit v1 on v0

--- a/solution.py
+++ b/solution.py
@@ -98,7 +98,7 @@
     local_weight = jnp.dot(
         features.astype(jnp.float32).T, back_rows, precision=lax.Precision.HIGHEST
     )
-    weight_grad = lax.psum(local_weight, ("rows", "rep")) * (1.0 / math.sqrt(node_total))
+    weight_grad = lax.psum(lax.psum(local_weight, "rep"), "rows") * (1.0 / math.sqrt(node_total))
     input_grad = jnp.dot(
         back_rows.astype(jnp.bfloat16), weight.T, preferred_element_type=jnp.float32
     ).astype(jnp.bfloat16)

time: 756 us -> 732 us (0.968)
  waiting for transfers between devices: 615 us -> 589 us
    psum x1 -> x2, waiting for transfers between devices: 246 us -> 218 us  [the longest x1 178 us: on_device(): lax.psum(lax.psum(local_weight, 'rep'), 'rows')]
  transfers between devices with their start and end apart: 5 -> 6, of which waited for: 5 -> 6; matrix products, arithmetic and copies ran while one was open for 2% -> 2% of each run, Pallas kernels for 0% -> 0%
where the time goes in v1:
time: 732 us; the launch traced here: 729 us
  waiting for transfers between devices  589 us (80%)
  local copies, waits for them, and re-layouts  48.9 us (7%)
  other arithmetic  29.3 us (4%)
  starting transfers between devices  28.8 us (4%)
  matrix products  19.3 us (3%)
  between operations  13.9 us (2%)
    psum x1, waiting for transfers between devices, on_device(): lax.psum(lax.psum(local_weight, 'rep'), 'rows')  178 us
    all_to_all x1, waiting for transfers between devices, on_device(): lax.all_to_all(outgoing, 'rows', split_axis=0, concat_axis=0, tiled=True)  177 us
    all_to_all x1, waiting for transfers between devices, on_device(): lax.all_to_all(serve_blocks(mixed_rows, asked_places, block_size), 'rows'...  93.1 us
    psum x1, waiting for transfers between devices, on_device(): summed = lax.psum(partial_sum, 'rep')  92.9 us
    psum x1, waiting for transfers between devices, on_device(): lax.psum(local_weight, 'rep')  40.2 us
    unnamed x14, local copies, waits for them, and re-layouts  19.2 us
  transfers between devices with their start and end apart: 6, of which 6 were waited for; matrix products, arithmetic and copies ran while one was open for 2% of the time, Pallas kernels for 0%

profile of v1, /device:TPU:2, one launch (start us, length us, event | category | flops | bytes accessed | tf_op | source)
XLA Modules:
  0.0 729.1 jit_solution(2726750308626880181)
XLA Ops:
  9.3 12.1 %all-to-all-start = ((s32[64,1,1]{2,1,0:T(1,128)}), s32[64,1,1]{2,1,0:T(1,128)S(1)}, u32[]{:S(2)}, u32[]{:S(2)}) async-start(s32[64,1,1]{2,1,0:T(1,128)} %copy.38), calls=%async_computation | async-start | bytes 65536 | tf_op jit(solution)/shard_map/all_to_all | solution.py:54
  22.7 8.2 %all-to-all-done = s32[64,1,1]{2,1,0:T(1,128)S(1)} async-done(((s32[64,1,1]{2,1,0:T(1,128)}), s32[64,1,1]{2,1,0:T(1,128)S(1)}, u32[]{:S(2)}, u32[]{:S(2)}) %all-to-all-start) | async-done | bytes 288 | tf_op jit(solution)/shard_map/all_to_all | solution.py:54
  32.1 2.8 gather_fusion.2
  36.1 4.0 select_select_fusion.2
  40.1 5.7 all-to-all-start.1
  46.1 2.8 gather_fusion.3
  48.9 93.1 %all-to-all-done.1 = bf16[64,128,256]{2,1,0:T(8,128)(2,1)} async-done(((bf16[64,128,256]{2,1,0:T(8,128)(2,1)}), bf16[64,128,256]{2,1,0:T(8,128)(2,1)}, u32[]{:S(2)}, u32[]{:S(2)}) %all-to-all-start.1) | async-done | bytes 4194336 | tf_op jit(solution)/shard_map/all_to_all | solution.py:56
  142.0 5.0 gather_fusion
  147.0 4.1 select_select_fusion.1
  151.0 2.8 fusion.2
  154.0 92.9 %all-reduce.4.cloned.1.call-done = f32[4096,256]{1,0:T(8,128)} async-done(((f32[4096,256]{1,0:T(8,128)}), f32[4096,256]{1,0:T(8,128)}) %all-reduce.4.cloned.1.call-update) | async-done | bytes 4194320 | tf_op jit(solution)/shard_map/psum | solution.py:70
  246.9 6.4 multiply_convert_fusion
  253.3 4.5 fusion
  257.9 9.0 %copy.41 = f32[64,128,256]{2,1,0:T(8,128)} copy(f32[64,128,256]{1,2,0:T(8,128)} %bitcast.59) | data formatting | bytes 16777216 | tf_op jit(solution)/shard_map/reshape | solution.py:79
  266.9 7.7 %gather_fusion.1 = f32[64,128,256]{2,1,0:T(8,128)} fusion(f32[64,128,256]{2,1,0:T(8,128)} %copy.41, s32[1024]{0:T(1024)S(1)} %pad_clamp_fusion), kind=kCustom, calls=%fused_computation.3 | custom fusion | bytes 16777472 | tf_op jit(solution)/shard_map/jit(_take)/gather | solution.py:83
  274.5 8.5 %select_select_fusion = f32[64,128,256]{2,1,0:T(8,128)} fusion(f32[64,128,256]{2,1,0:T(8,128)} %gather_fusion.1, pred[64]{0:T(512)(128)(4,1)S(1)} %compare_and_fusion.2, pred[64]{0:T(512)(128)(4,1)S(1)} %fusion.6), kind=kLoop, calls=%fused_computation.5 | loop fusion | flops 4194304 | bytes 16777344 | tf_op jit(solution)/shard_map/jit(_where)/select_n | solution.py:82
  283.0 10.7 %all-to-all-start.2 = ((f32[64,128,256]{2,1,0:T(8,128)}), f32[64,128,256]{2,1,0:T(8,128)}, u32[]{:S(2)}, u32[]{:S(2)}) async-start(f32[64,128,256]{2,1,0:T(8,128)} %select_select_fusion), calls=%async_computation.2 | async-start | bytes 16777216 | tf_op jit(solution)/shard_map/all_to_all | solution.py:85
  293.8 9.2 %copy.49 = f32[8,8,128,256]{3,1,2,0:T(8,128)} copy(f32[8,8,128,256]{2,3,1,0:T(8,128)} %bitcast.60) | data formatting | bytes 16777216
  303.0 176.8 %all-to-all-done.2 = f32[64,128,256]{2,1,0:T(8,128)} async-done(((f32[64,128,256]{2,1,0:T(8,128)}), f32[64,128,256]{2,1,0:T(8,128)}, u32[]{:S(2)}, u32[]{:S(2)}) %all-to-all-start.2) | async-done | bytes 8388640 | tf_op jit(solution)/shard_map/all_to_all | solution.py:85
  479.9 8.3 %copy.48 = f32[8,8,128,256]{3,1,2,0:T(8,128)S(1)} copy(f32[8,8,128,256]{3,2,1,0:T(8,128)} %bitcast.25) | data formatting | bytes 16777216
  488.1 2.9 fusion.8
  491.0 3.9 convolution_add_fusion
  501.7 40.2 %all-reduce.6.cloned.1.call-done = f32[256,256]{0,1:T(8,128)} async-done(((f32[256,256]{0,1:T(8,128)}), f32[256,256]{0,1:T(8,128)}) %all-reduce.6.cloned.1.call-update) | async-done | bytes 262160 | tf_op jit(solution)/shard_map/psum | solution.py:101
  543.1 177.7 %all-reduce.8.cloned.1.call-done = f32[256,256]{0,1:T(8,128)} async-done(((f32[256,256]{0,1:T(8,128)}), f32[256,256]{0,1:T(8,128)}) %all-reduce.8.cloned.1.call-update) | async-done | bytes 262160 | tf_op jit(solution)/shard_map/psum | solution.py:101
  (45 shorter events, 16.1 us)
Async XLA Ops:
  7.2 143.9 %copy-start = (bf16[32,1,2,128,128]{4,3,2,1,0:T(8,128)(2,1)S(1)}, bf16[32,1,2,128,128]{4,3,2,1,0:T(8,128)(2,1)}, u32[]{:S(2)}) copy-start(bf16[32,1,2,128,128]{4,3,2,1,0:T(8,128)(2,1)} %param.10) | copy-start | bytes 6291460
  9.3 21.6 %all-to-all-start = ((s32[64,1,1]{2,1,0:T(1,128)}), s32[64,1,1]{2,1,0:T(1,128)S(1)}, u32[]{:S(2)}, u32[]{:S(2)}) async-start(s32[64,1,1]{2,1,0:T(1,128)} %copy.38), calls=%async_computation | async-start | bytes 65536 | tf_op jit(solution)/shard_map/all_to_all | solution.py:54
  40.1 101.9 %all-to-all-start.1 = ((bf16[64,128,256]{2,1,0:T(8,128)(2,1)}), bf16[64,128,256]{2,1,0:T(8,128)(2,1)}, u32[]{:S(2)}, u32[]{:S(2)}) async-start(bf16[64,128,256]{2,1,0:T(8,128)(2,1)} %select_select_fusion.2), calls=%async_computation.1 | async-start | bytes 8388608 | tf_op jit(solution)/shard_map/all_to_all | solution.py:56
  45.8 201.1 %all-reduce.4.cloned.1.call-start = ((), (), s32[]{:S(2)}) async-start(), calls=%async_computation.3 | async-start | bytes 8388608 | tf_op jit(solution)/shard_map/psum | solution.py:70
  283.0 196.8 %all-to-all-start.2 = ((f32[64,128,256]{2,1,0:T(8,128)}), f32[64,128,256]{2,1,0:T(8,128)}, u32[]{:S(2)}, u32[]{:S(2)}) async-start(f32[64,128,256]{2,1,0:T(8,128)} %select_select_fusion), calls=%async_computation.2 | async-start | bytes 16777216 | tf_op jit(solution)/shard_map/all_to_all | solution.py:85
  293.8 248.1 %all-reduce.6.cloned.1.call-start = ((), (), s32[]{:S(2)}) async-start(), calls=%async_computation.4 | async-start | bytes 524288 | tf_op jit(solution)/shard_map/psum | solution.py:101
  479.8 11.2 %slice-start = ((s8[8388608]{0:T(1024)(128)(4,1)}), s8[4194304]{0:T(1024)(128)(4,1)S(1)}, s32[]{:S(2)}) async-start(s8[8388608]{0:T(1024)(128)(4,1)} %bitcast.63), calls=%async_computation.6 | async-start | bytes 8388608
  479.9 11.2 %slice-start.1 = ((s8[8388608]{0:T(1024)(128)(4,1)}), s8[4194304]{0:T(1024)(128)(4,1)S(1)}, s32[]{:S(2)}) async-start(s8[8388608]{0:T(1024)(128)(4,1)} %bitcast.63), calls=%async_computation.7 | async-start | bytes 8388608
  494.9 47.0 %copy-start.2 = (bf16[256,256]{1,0:T(8,128)(2,1)S(1)}, bf16[256,256]{1,0:T(8,128)(2,1)}, u32[]{:S(2)}) copy-start(bf16[256,256]{1,0:T(8,128)(2,1)} %param.8) | copy-start | bytes 393220
  494.9 227.7 %copy-start.1 = (bf16[32,1,2,128,128]{4,3,2,1,0:T(8,128)(2,1)S(1)}, bf16[32,1,2,128,128]{4,3,2,1,0:T(8,128)(2,1)}, u32[]{:S(2)}) copy-start(bf16[32,1,2,128,128]{4,3,2,1,0:T(8,128)(2,1)} %param.10) | copy-start | bytes 6291460
  499.2 221.6 %all-reduce.8.cloned.1.call-start = ((), (), s32[]{:S(2)}) async-start(), calls=%async_computation.5 | async-start | bytes 524288 | tf_op jit(solution)/shard_map/psum | solution.py:101
Sparse Core Ops, SparseCore 0:
  154.0 92.8 all-reduce.3
  499.4 42.4 all-reduce.5
  545.4 175.3 all-reduce.7
